TPU v7x, 32 devices: a whole 2x2x4 slice. The times are simulated.
32 devices in a mesh: grid: 8 (over z, core), tp: 4 (over y, x).
Axes of the slice: x: 2, y: 2, z: 4, core: 2. Of those that a mesh axis runs over, the one named last changes fastest.
Arguments:
- latents: bfloat16 [3072, 3072], P('grid'), may hold values from -6 to 6
- input_weight: bfloat16 [3072, 1536], P('grid', 'tp'), as said below
- norm_gains: float32 [2, 128], replicated, as said below
- text_pairs: bfloat16 [256, 1024], P(None, 'tp'), may hold values from -6 to 6
- text_count: int32 [1], replicated, may hold values from 64 to 256
- output_weight: bfloat16 [512, 3072], P('tp', 'grid'), may hold values from -0.25 to 0.25
Outputs:
- block_output: bfloat16 [3072, 3072], P('grid', 'tp')
Inputs may be any that keep to these rules, and one draw needn't show every extreme that they name: `text_count`: number of valid text tokens; the remaining text slots are padding. `input_weight`: a projection scaled by its fan-in. `norm_gains`: positive gains.
All inputs are finite; a program needn't handle non-finite values.
Results may differ from a plain program's by a relative error of at most 0.015.
Values may be sent and summed in bfloat16 or wider, within the bound.
No kernel may reach another device: no remote copies, remote signals or barrier semaphores. Data moves between devices by JAX's collectives and lax.ppermute only.
A program may use at most 64 MiB of HBM per device.

v0:
```python
import jax
import jax.numpy as jnp
import numpy as np
from jax import lax
from jax.sharding import PartitionSpec as P

GRID_H = 4
TILE = 384
epsilon = 1e-06


def shifted(x, axis, by):
    length = lax.axis_size(axis)
    pairs = [(i, i + by) for i in range(length) if 0 <= i + by < length]
    return lax.ppermute(x, axis, pairs)


def root_norm(values, gain):
    return values * lax.rsqrt(jnp.mean(values * values, axis=-1, keepdims=True) + epsilon) * gain


def local(latents, input_weight, norm_gains, text_pairs, text_count, output_weight):
    row_count = latents.shape[0]
    in_width = input_weight.shape[1]
    head_size = norm_gains.shape[1]
    head_count = in_width // (3 * head_size)
    tile_rows = TILE
    tiles_wide = row_count // tile_rows
    projected = jnp.dot(
        latents,
        lax.all_gather(input_weight, "grid", axis=0, tiled=True),
        preferred_element_type=jnp.float32,
    )
    projected = projected.reshape(row_count, head_count, 3, head_size)
    queries = root_norm(projected[:, :, 0], norm_gains[0]).astype(jnp.bfloat16)
    key_rows = root_norm(projected[:, :, 1], norm_gains[1]).astype(jnp.bfloat16)
    values = projected[:, :, 2].astype(jnp.bfloat16)
    stacked = jnp.concatenate(
        [
            key_rows.reshape(row_count, head_count * head_size),
            values.reshape(row_count, head_count * head_size),
        ],
        axis=1,
    )
    offsets = [(step_time, step_height) for step_time in (-1, 0, 1) for step_height in (-1, 0, 1)]
    neighbours = []
    for step_time, step_height in offsets:
        if step_time == 0 and step_height == 0:
            neighbours.append(stacked)
        else:
            neighbours.append(shifted(stacked, "grid", -(step_time * GRID_H + step_height)))
    planes = jnp.stack(neighbours)
    grid_time = lax.axis_size("grid") // GRID_H
    place = lax.axis_index("grid")
    time_here = place // GRID_H
    height_here = place % GRID_H
    plane_ok = jnp.stack(
        [
            (time_here + step_time >= 0)
            & (time_here + step_time < grid_time)
            & ((height_here + step_height >= 0) & (height_here + step_height < GRID_H))
            for step_time, step_height in offsets
        ]
    )
    width_keep = min(3, tiles_wide)
    starts = np.clip(np.arange(tiles_wide) - 1, 0, tiles_wide - width_keep)
    width_index = starts[:, None] + np.arange(width_keep)[None, :]
    width_ok = np.abs(width_index - np.arange(tiles_wide)[:, None]) <= 1
    window_rows = 9 * width_keep * tile_rows
    planes = planes.reshape(9, tiles_wide, tile_rows, 2 * head_count * head_size)
    window = (
        planes[:, width_index]
        .transpose(1, 0, 2, 3, 4)
        .reshape(tiles_wide, window_rows, 2, head_count, head_size)
    )
    key_window = window[:, :, 0]
    value_window = window[:, :, 1]
    live = plane_ok[None, :, None, None] & jnp.asarray(width_ok)[:, None, :, None]
    live = jnp.broadcast_to(live, (tiles_wide, 9, width_keep, tile_rows)).reshape(
        tiles_wide, window_rows
    )
    text = text_pairs.reshape(text_pairs.shape[0], head_count, 2, head_size)
    text_keys = root_norm(text[:, :, 0].astype(jnp.float32), norm_gains[1]).astype(jnp.bfloat16)
    text_values = text[:, :, 1]
    live_text = jnp.arange(text_pairs.shape[0]) < text_count[0]
    score_scale = head_size ** (-0.5)
    query_tiles = queries.reshape(tiles_wide, tile_rows, head_count, head_size)
    video_scores = (
        jnp.einsum("wqhd,wkhd->whqk", query_tiles, key_window, preferred_element_type=jnp.float32)
        * score_scale
    )
    text_scores = (
        jnp.einsum("wqhd,khd->whqk", query_tiles, text_keys, preferred_element_type=jnp.float32)
        * score_scale
    )
    video_scores = jnp.where(live[:, None, None, :], video_scores, -jnp.inf)
    text_scores = jnp.where(live_text[None, None, None, :], text_scores, -jnp.inf)
    row_max = jnp.maximum(video_scores.max(-1), text_scores.max(-1))[..., None]
    video_exp = jnp.exp(video_scores - row_max)
    text_exp = jnp.exp(text_scores - row_max)
    denominator = video_exp.sum(-1, keepdims=True) + text_exp.sum(-1, keepdims=True)
    video_weights = (video_exp / denominator).astype(jnp.bfloat16)
    text_weights = (text_exp / denominator).astype(jnp.bfloat16)
    mixed = jnp.einsum(
        "whqk,wkhd->wqhd", video_weights, value_window, preferred_element_type=jnp.float32
    )
    mixed = mixed + jnp.einsum(
        "whqk,khd->wqhd", text_weights, text_values, preferred_element_type=jnp.float32
    )
    attention = mixed.astype(jnp.bfloat16).reshape(row_count, head_count * head_size)
    term = jnp.dot(
        attention,
        lax.all_gather(output_weight, "grid", axis=1, tiled=True),
        preferred_element_type=jnp.float32,
    )
    return lax.psum_scatter(term.astype(jnp.bfloat16), "tp", scatter_dimension=1, tiled=True)


def solution(mesh):
    placed = (P("grid", None), P("grid", "tp"), P(), P(None, "tp"), P(), P("tp", "grid"))
    return jax.shard_map(
        local, mesh=mesh, in_specs=placed, out_specs=P("grid", "tp"), check_vma=False
    )
```

profile of v0, /device:TPU:0, one launch (start us, length us, event | category | flops | bytes accessed | tf_op | source)
XLA Modules:
  0.0 153.9 jit_solution(12105154632013553771)
XLA Ops:
  6.5 0.0 copy-start
  6.5 0.0 all-gather.2.cloned.1.call-start
  6.5 0.7 all-gather.2.cloned.1.call-update
  7.3 0.0 reduce-scatter.2.cloned.1.call-start
  7.4 0.1 stack.79
  7.5 0.1 broadcast_in_dim.44
  7.6 1.0 copy.16
  8.6 0.0 copy-start.4
  9.3 0.5 iota_compare_fusion
  9.8 0.8 slice_bitcast_fusion.2
  10.6 0.6 add_rsqrt_fusion.2
  11.2 21.6 %all_gather.7 = bf16[128,3072]{1,0:T(8,128)(2,1)} all-gather(bf16[128,384]{1,0:T(8,128)(2,1)} %param.14), channel_id=1, replica_groups=mesh['grid'=8,'tp'=4] {'grid'}, dimensions={1}, use_global_device_ids=true | all-gather | bytes 884736 | tf_op jit(solution)/shard_map/all_gather | solution.py:113
  32.8 0.0 copy-done.4
  32.8 13.9 %all-gather.2.cloned.1.call-done = bf16[3072,384]{1,0:T(8,128)(2,1)} async-done(((bf16[384,384]{1,0:T(8,128)(2,1)}), bf16[3072,384]{1,0:T(8,128)(2,1)}) %all-gather.2.cloned.1.call-update) | async-done | bytes 2359312 | tf_op jit(solution)/shard_map/all_gather | solution.py:31
  46.6 0.0 copy-done
  46.7 3.1 %fusion.34 = f32[384,384]{0,1:T(8,128)S(1)} fusion(bf16[384,3072]{1,0:T(8,128)(2,1)S(1)} %copy-done, bf16[3072,384]{1,0:T(8,128)(2,1)} %all-gather.2.cloned.1.call-done), kind=kOutput, calls=%fused_computation.61 | convolution fusion | flops 905969664 | bytes 5308416 | tf_op jit(solution)/shard_map/dot_general | solution.py:29
  49.8 0.1 copy.23
  49.9 0.1 multiply_reduce_fusion.1
  50.1 0.1 copy.24
  50.2 0.1 fusion.18
  50.4 3.1 %collective-permute-start = (bf16[384,256]{1,0:T(8,128)(2,1)S(1)}, bf16[384,256]{1,0:T(8,128)(2,1)S(1)}, u32[]{:S(2)}, u32[]{:S(2)}) collective-permute-start(bf16[384,256]{1,0:T(8,128)(2,1)S(1)} %pad_maximum_fusion), channel_id=1, source_target_pairs={{0,20},{4,24},{8,28},{1,21},{5,25},{9,29},{2,22},{6,26},{10,30},{3... | collective-permute-start | bytes 589832 | tf_op jit(solution)/shard_map/ppermute | solution.py:15
  53.5 1.3 collective-permute-start.1
  54.8 2.3 %collective-permute-start.2 = (bf16[384,256]{1,0:T(8,128)(2,1)S(1)}, bf16[384,256]{1,0:T(8,128)(2,1)S(1)}, u32[]{:S(2)}, u32[]{:S(2)}) collective-permute-start(bf16[384,256]{1,0:T(8,128)(2,1)S(1)} %pad_maximum_fusion), channel_id=1, source_target_pairs={{0,12},{4,16},{8,20},{12,24},{16,28},{1,13},{5,17},{9,21},{13,25},... | collective-permute-start | bytes 589832 | tf_op jit(solution)/shard_map/ppermute | solution.py:15
  57.1 1.3 collective-permute-start.3
  58.4 1.3 collective-permute-start.4
  59.7 1.9 %fusion.33 = (f32[384]{0:T(512)S(1)}, f32[1,256,1,384]{3,1,2,0:T(8,128)}) fusion(f32[384,1,3,128]{0,3,2,1:T(8,128)S(1)} %bitcast.111, f32[128]{0:T(128)S(1)} %get-tuple-element.9, f32[384]{0:T(512)S(1)} %add_rsqrt_fusion, f32[128]{0:T(128)S(1)} %get-tuple-element.10, f32[256]{0:T(256)} %add_rsqrt_fusion.2, bf16[256,1,2,128]{0,3,2,1:T(8,128)(2,1)} %bitcast.114, ...), kind=kOutput, calls=%fused_computation.60 | convolution fusion | flops 25738880 | bytes 661504 | tf_op jit(solution)/shard_map/wqhd,khd->whqk/dot_general | solution.py:93
  61.6 0.0 collective-permute-done
  61.6 1.3 collective-permute-start.5
  62.9 0.7 bitcast_dynamic-update-slice_fusion.8
  63.6 0.0 collective-permute-done.1
  63.6 1.3 collective-permute-start.6
  64.9 0.7 bitcast_dynamic-update-slice_fusion.7
  65.6 1.6 %collective-permute-done.2 = bf16[384,256]{1,0:T(8,128)(2,1)S(1)} collective-permute-done((bf16[384,256]{1,0:T(8,128)(2,1)S(1)}, bf16[384,256]{1,0:T(8,128)(2,1)S(1)}, u32[]{:S(2)}, u32[]{:S(2)}) %collective-permute-start.2) | collective-permute-done | bytes 196640 | tf_op jit(solution)/shard_map/ppermute | solution.py:15
  67.2 1.3 collective-permute-start.7
  68.5 0.7 bitcast_dynamic-update-slice_fusion.6
  69.2 0.0 collective-permute-done.3
  69.2 0.7 bitcast_dynamic-update-slice_fusion.5
  69.9 0.7 bitcast_dynamic-update-slice_fusion.4
  70.6 0.0 collective-permute-done.4
  70.6 0.7 bitcast_dynamic-update-slice_fusion.3
  71.3 0.0 collective-permute-done.5
  71.3 0.7 bitcast_dynamic-update-slice_fusion.2
  72.0 6.6 %collective-permute-done.6 = bf16[384,256]{1,0:T(8,128)(2,1)S(1)} collective-permute-done((bf16[384,256]{1,0:T(8,128)(2,1)S(1)}, bf16[384,256]{1,0:T(8,128)(2,1)S(1)}, u32[]{:S(2)}, u32[]{:S(2)}) %collective-permute-start.6) | collective-permute-done | bytes 196640 | tf_op jit(solution)/shard_map/ppermute | solution.py:15
  78.6 0.7 bitcast_dynamic-update-slice_fusion.1
  79.3 10.5 %collective-permute-done.7 = bf16[384,256]{1,0:T(8,128)(2,1)S(1)} collective-permute-done((bf16[384,256]{1,0:T(8,128)(2,1)S(1)}, bf16[384,256]{1,0:T(8,128)(2,1)S(1)}, u32[]{:S(2)}, u32[]{:S(2)}) %collective-permute-start.7) | collective-permute-done | bytes 196640 | tf_op jit(solution)/shard_map/ppermute | solution.py:15
  89.8 0.7 bitcast_dynamic-update-slice_fusion
  90.5 4.5 %reshape_transpose.3 = bf16[1,3456,2,1,128]{4,2,1,3,0:T(2,128)(2,1)} reshape(bf16[9,384,256]{2,1,0:T(8,128)(2,1)} %bitcast_dynamic-update-slice_fusion) | data formatting | bytes 3538944 | tf_op jit(solution)/shard_map/reshape;transpose | solution.py:74
  95.0 5.8 %fusion.30 = (bf16[1,3456,1,1,128]{4,2,1,3,0:T(2,128)(2,1)}, bf16[1,3456,1,1,128]{4,2,1,3,0:T(2,128)(2,1)S(1)}) fusion(bf16[1,3456,2,1,128]{4,2,1,3,0:T(2,128)(2,1)} %reshape_transpose.3), kind=kLoop, calls=%fused_computation.57 | loop fusion | bytes 3538944 | tf_op jit(solution)/shard_map/slice | solution.py:77
  100.8 0.0 copy-start.3
  100.8 1.1 fusion.32
  101.9 0.0 copy-start.1
  101.9 0.0 copy-done.3
  102.0 0.1 fusion.15
  102.1 0.0 copy-start.5
  102.1 0.0 copy-start.2
  102.1 0.9 fusion.1
  102.9 1.3 copy-done.1
  104.3 0.0 copy-done.5
  104.3 0.2 convolution_bitcast_fusion
  104.5 0.0 copy-done.2
  104.5 6.8 %convolution_convert_fusion = bf16[384,3072]{1,0:T(8,128)(2,1)} fusion(bf16[128,3072]{1,0:T(8,128)(2,1)S(1)} %copy-done.2, f32[1,384,1,128]{1,3,2,0:T(8,128)S(1)} %convolution_bitcast_fusion, f32[384,3456]{1,0:T(8,128)} %copy-done.1, f32[384]{0:T(512)S(1)} %add.90, f32[384]{0:T(512)S(1)} %max.9, bf16[1,3456,1,1,128]{4,2,1,3,0:T(2,128)(2,1)} %get-tuple-element.5), kind=kOutput, calls=%fused_computation.5 | convolution fusion | flops 646987776 | bytes 9538560 | tf_op jit(solution)/shard_map/dot_general | solution.py:111
  111.3 0.0 reduce-scatter.2.cloned.1.call-update
  111.3 35.7 %reduce-scatter.2.cloned.1.call-done = bf16[384,768]{1,0:T(8,128)(2,1)} async-done(((bf16[384,3072]{1,0:T(8,128)(2,1)}), bf16[384,768]{1,0:T(8,128)(2,1)}) %reduce-scatter.2.cloned.1.call-update) | async-done | bytes 589840 | tf_op jit(solution)/shard_map/reduce_scatter | solution.py:116
  (9 shorter events, 0.2 us)
Async XLA Ops:
  6.5 40.1 %copy-start = (bf16[384,3072]{1,0:T(8,128)(2,1)S(1)}, bf16[384,3072]{1,0:T(8,128)(2,1)}, u32[]{:S(2)}) copy-start(bf16[384,3072]{1,0:T(8,128)(2,1)} %param.9) | copy-start | bytes 7077892
  6.5 40.1 %all-gather.2.cloned.1.call-start = ((), (), s32[]{:S(2)}) async-start(), calls=%async_computation.1 | async-start | bytes 2654208 | tf_op jit(solution)/shard_map/all_gather | solution.py:31
  7.3 139.8 %reduce-scatter.2.cloned.1.call-start = ((), (), s32[]{:S(2)}) async-start(), calls=%async_computation.2 | async-start | bytes 2949120 | tf_op jit(solution)/shard_map/reduce_scatter | solution.py:116
  8.6 24.2 %copy-start.4 = (bf16[256,256]{0,1:T(8,128)(2,1)}, bf16[256,256]{0,1:T(8,128)(2,1)S(1)}, u32[]{:S(2)}) copy-start(bf16[256,256]{0,1:T(8,128)(2,1)S(1)} %copy.16) | copy-start | bytes 393220
  50.4 11.3 %collective-permute-start = (bf16[384,256]{1,0:T(8,128)(2,1)S(1)}, bf16[384,256]{1,0:T(8,128)(2,1)S(1)}, u32[]{:S(2)}, u32[]{:S(2)}) collective-permute-start(bf16[384,256]{1,0:T(8,128)(2,1)S(1)} %pad_maximum_fusion), channel_id=1, source_target_pairs={{0,20},{4,24},{8,28},{1,21},{5,25},{9,29},{2,22},{6,26},{10,30},{3... | collective-permute-start | bytes 589832 | tf_op jit(solution)/shard_map/ppermute | solution.py:15
  53.5 10.1 %collective-permute-start.1 = (bf16[384,256]{1,0:T(8,128)(2,1)S(1)}, bf16[384,256]{1,0:T(8,128)(2,1)S(1)}, u32[]{:S(2)}, u32[]{:S(2)}) collective-permute-start(bf16[384,256]{1,0:T(8,128)(2,1)S(1)} %pad_maximum_fusion), channel_id=1, source_target_pairs={{0,16},{4,20},{8,24},{12,28},{1,17},{5,21},{9,25},{13,29},{2,18},{... | collective-permute-start | bytes 589832 | tf_op jit(solution)/shard_map/ppermute | solution.py:15
  54.8 12.4 %collective-permute-start.2 = (bf16[384,256]{1,0:T(8,128)(2,1)S(1)}, bf16[384,256]{1,0:T(8,128)(2,1)S(1)}, u32[]{:S(2)}, u32[]{:S(2)}) collective-permute-start(bf16[384,256]{1,0:T(8,128)(2,1)S(1)} %pad_maximum_fusion), channel_id=1, source_target_pairs={{0,12},{4,16},{8,20},{12,24},{16,28},{1,13},{5,17},{9,21},{13,25},... | collective-permute-start | bytes 589832 | tf_op jit(solution)/shard_map/ppermute | solution.py:15
  57.1 12.1 %collective-permute-start.3 = (bf16[384,256]{1,0:T(8,128)(2,1)S(1)}, bf16[384,256]{1,0:T(8,128)(2,1)S(1)}, u32[]{:S(2)}, u32[]{:S(2)}) collective-permute-start(bf16[384,256]{1,0:T(8,128)(2,1)S(1)} %pad_maximum_fusion), channel_id=1, source_target_pairs={{0,4},{4,8},{8,12},{12,16},{16,20},{20,24},{24,28},{1,5},{5,9},{9,... | collective-permute-start | bytes 589832 | tf_op jit(solution)/shard_map/ppermute | solution.py:15
  58.4 12.2 %collective-permute-start.4 = (bf16[384,256]{1,0:T(8,128)(2,1)S(1)}, bf16[384,256]{1,0:T(8,128)(2,1)S(1)}, u32[]{:S(2)}, u32[]{:S(2)}) collective-permute-start(bf16[384,256]{1,0:T(8,128)(2,1)S(1)} %pad_maximum_fusion), channel_id=1, source_target_pairs={{4,0},{8,4},{12,8},{16,12},{20,16},{24,20},{28,24},{5,1},{9,5},{13... | collective-permute-start | bytes 589832 | tf_op jit(solution)/shard_map/ppermute | solution.py:15
  61.6 9.6 %collective-permute-start.5 = (bf16[384,256]{1,0:T(8,128)(2,1)S(1)}, bf16[384,256]{1,0:T(8,128)(2,1)S(1)}, u32[]{:S(2)}, u32[]{:S(2)}) collective-permute-start(bf16[384,256]{1,0:T(8,128)(2,1)S(1)} %pad_maximum_fusion), channel_id=1, source_target_pairs={{12,0},{16,4},{20,8},{24,12},{28,16},{13,1},{17,5},{21,9},{25,13},... | collective-permute-start | bytes 589832 | tf_op jit(solution)/shard_map/ppermute | solution.py:15
  63.6 15.0 %collective-permute-start.6 = (bf16[384,256]{1,0:T(8,128)(2,1)S(1)}, bf16[384,256]{1,0:T(8,128)(2,1)S(1)}, u32[]{:S(2)}, u32[]{:S(2)}) collective-permute-start(bf16[384,256]{1,0:T(8,128)(2,1)S(1)} %pad_maximum_fusion), channel_id=1, source_target_pairs={{16,0},{20,4},{24,8},{28,12},{17,1},{21,5},{25,9},{29,13},{18,2},{... | collective-permute-start | bytes 589832 | tf_op jit(solution)/shard_map/ppermute | solution.py:15
  67.2 22.6 %collective-permute-start.7 = (bf16[384,256]{1,0:T(8,128)(2,1)S(1)}, bf16[384,256]{1,0:T(8,128)(2,1)S(1)}, u32[]{:S(2)}, u32[]{:S(2)}) collective-permute-start(bf16[384,256]{1,0:T(8,128)(2,1)S(1)} %pad_maximum_fusion), channel_id=1, source_target_pairs={{20,0},{24,4},{28,8},{21,1},{25,5},{29,9},{22,2},{26,6},{30,10},{2... | collective-permute-start | bytes 589832 | tf_op jit(solution)/shard_map/ppermute | solution.py:15
  100.8 1.1 copy-start.3
  101.9 2.3 %copy-start.1 = (f32[384,3456]{1,0:T(8,128)}, f32[384,3456]{1,0:T(8,128)S(1)}, u32[]{:S(2)}) copy-start(f32[384,3456]{1,0:T(8,128)S(1)} %get-tuple-element.12) | copy-start | bytes 15925252
  102.1 2.2 %copy-start.5 = (bf16[256,256]{0,1:T(8,128)(2,1)S(1)}, bf16[256,256]{0,1:T(8,128)(2,1)}, u32[]{:S(2)}) copy-start(bf16[256,256]{0,1:T(8,128)(2,1)} %copy-done.4) | copy-start | bytes 393220
  102.1 2.4 %copy-start.2 = (bf16[128,3072]{1,0:T(8,128)(2,1)S(1)}, bf16[128,3072]{1,0:T(8,128)(2,1)}, u32[]{:S(2)}) copy-start(bf16[128,3072]{1,0:T(8,128)(2,1)} %all_gather.7) | copy-start | bytes 2359300
Sparse Core Ops, SparseCore 0:
  9.0 37.6 all-gather.1
  111.4 35.5 reduce-scatter.1
where the time goes:
time: 154 us
  waiting for transfers between devices  69.1 us (45%)
  blocking collectives  21.6 us (14%)
  local copies, waits for them, and re-layouts  19.4 us (13%)
  between operations  14.3 us (9%)
  starting transfers between devices  13.2 us (9%)
  matrix products  13.1 us (9%)
  other arithmetic  3.13 us (2%)
    reduce_scatter x1, waiting for transfers between devices, local(): lax.psum_scatter(term.astype(jnp.bfloat16), 'tp', scatter_dimension=1, ti...  35.7 us
    all_gather x1, blocking collectives, local(): lax.all_gather(output_weight, 'grid', axis=1, tiled=True)  21.6 us
    ppermute x8, waiting for transfers between devices, shifted(): return lax.ppermute(x, axis, pairs)  18.8 us
    all_gather x1, waiting for transfers between devices, local(): lax.all_gather(input_weight, 'grid', axis=0, tiled=True)  13.9 us
    ppermute x8, starting transfers between devices, shifted(): return lax.ppermute(x, axis, pairs)  13.1 us
    unnamed x22, local copies, waits for them, and re-layouts  7.46 us
    dot_general x1, matrix products, local(): jnp.dot(attention, lax.all_gather(output_weight, 'grid', axis=1, tiled=Tr...  6.76 us
    slice x1, local copies, waits for them, and re-layouts, local(): value_window = window[:, :, 1]  5.84 us
  transfers between devices with their start and end apart: 10, of which 5 were waited for; matrix products, arithmetic and copies ran while one was open for 7% of the time, Pallas kernels for 0%

commit v1 on v0

--- a/solution.py
+++ b/solution.py
@@ -110,7 +110,9 @@
     attention = mixed.astype(jnp.bfloat16).reshape(row_count, head_count * head_size)
     term = jnp.dot(
         attention,
-        lax.all_gather(output_weight, "grid", axis=1, tiled=True),
+        jnp.concatenate(
+            lax.all_to_all(jnp.stack([output_weight] * lax.axis_size("grid")), "grid", 0, 0), axis=1
+        ),
         preferred_element_type=jnp.float32,
     )
     return lax.psum_scatter(term.astype(jnp.bfloat16), "tp", scatter_dimension=1, tiled=True)

time: 154 us -> 165 us (1.071)
  waiting for transfers between devices: 69.1 us -> 94.3 us
  blocking collectives: 21.6 us -> 0 us
  starting transfers between devices: 13.2 us -> 19.4 us
    all_gather x1, waiting for transfers between devices: 13.9 us -> 39.1 us  [local(): lax.all_gather(input_weight, 'grid', axis=0, tiled=True)]
    all_gather x1 -> x0, blocking collectives: 21.6 us -> none  [local(): lax.all_gather(output_weight, 'grid', axis=1, tiled=True)]
    all_to_all x0 -> x1, starting transfers between devices: none -> 6.35 us  [local(): lax.all_to_all(jnp.stack([output_weight] * lax.axis_size('grid')), 'grid'...]
    unnamed x22 -> x25, local copies, waits for them, and re-layouts: 7.46 us -> 7.68 us
  transfers between devices with their start and end apart: 10 -> 11, of which waited for: 5 -> 5; matrix products, arithmetic and copies ran while one was open for 7% -> 17% of each run, Pallas kernels for 0% -> 0%
where the time goes in v1:
time: 165 us; the launch traced here: 164 us
  waiting for transfers between devices  94.3 us (57%)
  local copies, waits for them, and re-layouts  19.9 us (12%)
  starting transfers between devices  19.4 us (12%)
  between operations  14.3 us (9%)
  matrix products  13.2 us (8%)
  other arithmetic  3.2 us (2%)
    all_gather x1, waiting for transfers between devices, local(): lax.all_gather(input_weight, 'grid', axis=0, tiled=True)  39.1 us
    reduce_scatter x1, waiting for transfers between devices, local(): lax.psum_scatter(term.astype(jnp.bfloat16), 'tp', scatter_dimension=1, ti...  35.7 us
    ppermute x8, waiting for transfers between devices, shifted(): return lax.ppermute(x, axis, pairs)  18.7 us
    ppermute x8, starting transfers between devices, shifted(): return lax.ppermute(x, axis, pairs)  13 us
    unnamed x25, local copies, waits for them, and re-layouts  7.68 us
    dot_general x1, matrix products, local(): jnp.dot(attention, jnp.concatenate(lax.all_to_all(jnp.stack([output_weigh...  6.9 us
    all_to_all x1, starting transfers between devices, local(): lax.all_to_all(jnp.stack([output_weight] * lax.axis_size('grid')), 'grid'...  6.35 us
    slice x1, local copies, waits for them, and re-layouts, local(): value_window = window[:, :, 1]  5.84 us
  transfers between devices with their start and end apart: 11, of which 5 were waited for; matrix products, arithmetic and copies ran while one was open for 17% of the time, Pallas kernels for 0%

profile of v1, /device:TPU:0, one launch (start us, length us, event | category | flops | bytes accessed | tf_op | source)
XLA Modules:
  0.0 164.4 jit_solution(2568156918180116861)
XLA Ops:
  6.5 0.0 copy-start
  6.5 0.0 copy-start.5
  6.5 0.0 copy-start.6
  6.5 0.0 all-gather.2.cloned.1.call-start
  6.5 0.7 all-gather.2.cloned.1.call-update
  7.3 1.1 copy.21
  8.3 1.0 stack.91
  9.4 6.4 %all-to-all-start = ((bf16[8,128,384]{1,2,0:T(8,128)(2,1)}), bf16[8,128,384]{1,2,0:T(8,128)(2,1)}, u32[]{:S(2)}, u32[]{:S(2)}) async-start(bf16[8,128,384]{1,2,0:T(8,128)(2,1)} %stack.91), calls=%async_computation | async-start | bytes 1572864 | tf_op jit(solution)/shard_map/all_to_all | solution.py:114
  15.7 0.0 reduce-scatter.2.cloned.1.call-start
  15.8 0.1 stack.90
  15.9 0.1 broadcast_in_dim.44
  16.0 0.0 copy-done.5
  16.0 0.1 copy.17
  16.2 0.0 copy-start.3
  16.8 0.6 iota_compare_fusion
  17.4 0.0 copy-done.6
  17.4 0.6 add_rsqrt_fusion.2
  18.0 0.0 copy-done.3
  18.0 39.1 %all-gather.2.cloned.1.call-done = bf16[3072,384]{1,0:T(8,128)(2,1)} async-done(((bf16[384,384]{1,0:T(8,128)(2,1)}), bf16[3072,384]{1,0:T(8,128)(2,1)}) %all-gather.2.cloned.1.call-update) | async-done | bytes 2359312 | tf_op jit(solution)/shard_map/all_gather | solution.py:31
  57.1 0.0 copy-done
  57.1 3.1 %fusion.34 = f32[384,384]{0,1:T(8,128)S(1)} fusion(bf16[384,3072]{1,0:T(8,128)(2,1)S(1)} %copy-done, bf16[3072,384]{1,0:T(8,128)(2,1)} %all-gather.2.cloned.1.call-done), kind=kOutput, calls=%fused_computation.61 | convolution fusion | flops 905969664 | bytes 5308416 | tf_op jit(solution)/shard_map/dot_general | solution.py:29
  60.3 0.1 copy.25
  60.4 0.1 multiply_reduce_fusion.1
  60.6 0.1 copy.26
  60.7 0.1 fusion.18
  60.9 2.0 %collective-permute-start = (bf16[384,256]{1,0:T(8,128)(2,1)S(1)}, bf16[384,256]{1,0:T(8,128)(2,1)S(1)}, u32[]{:S(2)}, u32[]{:S(2)}) collective-permute-start(bf16[384,256]{1,0:T(8,128)(2,1)S(1)} %pad_maximum_fusion), channel_id=1, source_target_pairs={{0,20},{4,24},{8,28},{1,21},{5,25},{9,29},{2,22},{6,26},{10,30},{3... | collective-permute-start | bytes 589832 | tf_op jit(solution)/shard_map/ppermute | solution.py:15
  62.9 1.3 collective-permute-start.1
  64.2 3.2 %collective-permute-start.2 = (bf16[384,256]{1,0:T(8,128)(2,1)S(1)}, bf16[384,256]{1,0:T(8,128)(2,1)S(1)}, u32[]{:S(2)}, u32[]{:S(2)}) collective-permute-start(bf16[384,256]{1,0:T(8,128)(2,1)S(1)} %pad_maximum_fusion), channel_id=1, source_target_pairs={{0,12},{4,16},{8,20},{12,24},{16,28},{1,13},{5,17},{9,21},{13,25},... | collective-permute-start | bytes 589832 | tf_op jit(solution)/shard_map/ppermute | solution.py:15
  67.4 1.3 collective-permute-start.3
  68.8 1.3 collective-permute-start.4
  70.1 1.9 %fusion.33 = (f32[384]{0:T(512)S(1)}, f32[1,256,1,384]{3,1,2,0:T(8,128)}) fusion(f32[384,1,3,128]{0,3,2,1:T(8,128)S(1)} %bitcast.114, f32[128]{0:T(128)S(1)} %get-tuple-element.9, f32[384]{0:T(512)S(1)} %add_rsqrt_fusion, f32[128]{0:T(128)S(1)} %get-tuple-element.10, f32[256]{0:T(256)} %add_rsqrt_fusion.2, bf16[256,1,2,128]{0,3,2,1:T(8,128)(2,1)} %bitcast.117, ...), kind=kOutput, calls=%fused_computation.60 | convolution fusion | flops 25738880 | bytes 661504 | tf_op jit(solution)/shard_map/wqhd,khd->whqk/dot_general | solution.py:93
  72.0 0.0 collective-permute-done
  72.0 1.3 collective-permute-start.5
  73.3 0.7 bitcast_dynamic-update-slice_fusion.8
  74.0 0.0 collective-permute-done.1
  74.0 1.3 collective-permute-start.6
  75.3 0.7 bitcast_dynamic-update-slice_fusion.7
  76.0 0.1 collective-permute-done.2
  76.0 1.3 collective-permute-start.7
  77.3 0.7 bitcast_dynamic-update-slice_fusion.6
  78.0 0.0 collective-permute-done.3
  78.0 0.7 bitcast_dynamic-update-slice_fusion.5
  78.7 0.7 bitcast_dynamic-update-slice_fusion.4
  79.4 0.0 collective-permute-done.4
  79.4 0.7 bitcast_dynamic-update-slice_fusion.3
  80.1 0.0 collective-permute-done.5
  80.1 0.7 bitcast_dynamic-update-slice_fusion.2
  80.8 5.6 %collective-permute-done.6 = bf16[384,256]{1,0:T(8,128)(2,1)S(1)} collective-permute-done((bf16[384,256]{1,0:T(8,128)(2,1)S(1)}, bf16[384,256]{1,0:T(8,128)(2,1)S(1)}, u32[]{:S(2)}, u32[]{:S(2)}) %collective-permute-start.6) | collective-permute-done | bytes 196640 | tf_op jit(solution)/shard_map/ppermute | solution.py:15
  86.4 0.7 bitcast_dynamic-update-slice_fusion.1
  87.1 13.1 %collective-permute-done.7 = bf16[384,256]{1,0:T(8,128)(2,1)S(1)} collective-permute-done((bf16[384,256]{1,0:T(8,128)(2,1)S(1)}, bf16[384,256]{1,0:T(8,128)(2,1)S(1)}, u32[]{:S(2)}, u32[]{:S(2)}) %collective-permute-start.7) | collective-permute-done | bytes 196640 | tf_op jit(solution)/shard_map/ppermute | solution.py:15
  100.2 0.7 bitcast_dynamic-update-slice_fusion
  100.9 4.5 %reshape_transpose.3 = bf16[1,3456,2,1,128]{4,2,1,3,0:T(2,128)(2,1)} reshape(bf16[9,384,256]{2,1,0:T(8,128)(2,1)} %bitcast_dynamic-update-slice_fusion) | data formatting | bytes 3538944 | tf_op jit(solution)/shard_map/reshape;transpose | solution.py:74
  105.3 5.8 %fusion.30 = (bf16[1,3456,1,1,128]{4,2,1,3,0:T(2,128)(2,1)}, bf16[1,3456,1,1,128]{4,2,1,3,0:T(2,128)(2,1)S(1)}) fusion(bf16[1,3456,2,1,128]{4,2,1,3,0:T(2,128)(2,1)} %reshape_transpose.3), kind=kLoop, calls=%fused_computation.57 | loop fusion | bytes 3538944 | tf_op jit(solution)/shard_map/slice | solution.py:77
  111.2 1.1 fusion.32
  112.3 0.0 copy-done.2
  112.3 0.1 fusion.15
  112.4 0.9 fusion.1
  113.3 1.3 copy-done.1
  114.6 0.0 copy-done.4
  114.6 0.2 convolution_bitcast_fusion
  114.8 0.0 all-to-all-done
  114.9 6.9 %convolution_convert_fusion = bf16[384,3072]{1,0:T(8,128)(2,1)} fusion(bf16[128,3072]{0,1:T(8,128)(2,1)} %bitcast.38, f32[1,384,1,128]{1,3,2,0:T(8,128)S(1)} %convolution_bitcast_fusion, f32[384,3456]{1,0:T(8,128)} %copy-done.1, f32[384]{0:T(512)S(1)} %add.90, f32[384]{0:T(512)S(1)} %max.9, bf16[1,3456,1,1,128]{4,2,1,3,0:T(2,128)(2,1)} %get-tuple-element.5), kind=kOutput, calls=%fused_computation.5 | convolution fusion | flops 646987776 | bytes 9538560 | tf_op jit(solution)/shard_map/dot_general | solution.py:111
  121.7 0.0 reduce-scatter.2.cloned.1.call-update
  121.8 35.7 %reduce-scatter.2.cloned.1.call-done = bf16[384,768]{1,0:T(8,128)(2,1)} async-done(((bf16[384,3072]{1,0:T(8,128)(2,1)}), bf16[384,768]{1,0:T(8,128)(2,1)}) %reduce-scatter.2.cloned.1.call-update) | async-done | bytes 589840 | tf_op jit(solution)/shard_map/reduce_scatter | solution.py:118
  (13 shorter events, 0.2 us)
Async XLA Ops:
  6.5 50.6 %copy-start = (bf16[384,3072]{1,0:T(8,128)(2,1)S(1)}, bf16[384,3072]{1,0:T(8,128)(2,1)}, u32[]{:S(2)}) copy-start(bf16[384,3072]{1,0:T(8,128)(2,1)} %param.9) | copy-start | bytes 7077892
  6.5 9.5 %copy-start.5 = (bf16[256,256]{1,0:T(8,128)(2,1)S(1)}, bf16[256,256]{1,0:T(8,128)(2,1)}, u32[]{:S(2)}) copy-start(bf16[256,256]{1,0:T(8,128)(2,1)} %param.12) | copy-start | bytes 393220
  6.5 10.9 %copy-start.6 = (f32[2,128]{1,0:T(2,128)S(1)}, f32[2,128]{1,0:T(2,128)}, u32[]{:S(2)}) copy-start(f32[2,128]{1,0:T(2,128)} %param.11) | copy-start | bytes 3076
  6.5 50.6 %all-gather.2.cloned.1.call-start = ((), (), s32[]{:S(2)}) async-start(), calls=%async_computation.2 | async-start | bytes 2654208 | tf_op jit(solution)/shard_map/all_gather | solution.py:31
  9.4 105.5 %all-to-all-start = ((bf16[8,128,384]{1,2,0:T(8,128)(2,1)}), bf16[8,128,384]{1,2,0:T(8,128)(2,1)}, u32[]{:S(2)}, u32[]{:S(2)}) async-start(bf16[8,128,384]{1,2,0:T(8,128)(2,1)} %stack.91), calls=%async_computation | async-start | bytes 1572864 | tf_op jit(solution)/shard_map/all_to_all | solution.py:114
  15.7 141.8 %reduce-scatter.2.cloned.1.call-start = ((), (), s32[]{:S(2)}) async-start(), calls=%async_computation.3 | async-start | bytes 2949120 | tf_op jit(solution)/shard_map/reduce_scatter | solution.py:118
  16.2 1.9 %copy-start.3 = (bf16[256,256]{0,1:T(8,128)(2,1)}, bf16[256,256]{0,1:T(8,128)(2,1)S(1)}, u32[]{:S(2)}) copy-start(bf16[256,256]{0,1:T(8,128)(2,1)S(1)} %copy.17) | copy-start | bytes 393220
  60.9 11.1 %collective-permute-start = (bf16[384,256]{1,0:T(8,128)(2,1)S(1)}, bf16[384,256]{1,0:T(8,128)(2,1)S(1)}, u32[]{:S(2)}, u32[]{:S(2)}) collective-permute-start(bf16[384,256]{1,0:T(8,128)(2,1)S(1)} %pad_maximum_fusion), channel_id=1, source_target_pairs={{0,20},{4,24},{8,28},{1,21},{5,25},{9,29},{2,22},{6,26},{10,30},{3... | collective-permute-start | bytes 589832 | tf_op jit(solution)/shard_map/ppermute | solution.py:15
  62.9 11.0 %collective-permute-start.1 = (bf16[384,256]{1,0:T(8,128)(2,1)S(1)}, bf16[384,256]{1,0:T(8,128)(2,1)S(1)}, u32[]{:S(2)}, u32[]{:S(2)}) collective-permute-start(bf16[384,256]{1,0:T(8,128)(2,1)S(1)} %pad_maximum_fusion), channel_id=1, source_target_pairs={{0,16},{4,20},{8,24},{12,28},{1,17},{5,21},{9,25},{13,29},{2,18},{... | collective-permute-start | bytes 589832 | tf_op jit(solution)/shard_map/ppermute | solution.py:15
  64.2 11.8 %collective-permute-start.2 = (bf16[384,256]{1,0:T(8,128)(2,1)S(1)}, bf16[384,256]{1,0:T(8,128)(2,1)S(1)}, u32[]{:S(2)}, u32[]{:S(2)}) collective-permute-start(bf16[384,256]{1,0:T(8,128)(2,1)S(1)} %pad_maximum_fusion), channel_id=1, source_target_pairs={{0,12},{4,16},{8,20},{12,24},{16,28},{1,13},{5,17},{9,21},{13,25},... | collective-permute-start | bytes 589832 | tf_op jit(solution)/shard_map/ppermute | solution.py:15
  67.4 10.6 %collective-permute-start.3 = (bf16[384,256]{1,0:T(8,128)(2,1)S(1)}, bf16[384,256]{1,0:T(8,128)(2,1)S(1)}, u32[]{:S(2)}, u32[]{:S(2)}) collective-permute-start(bf16[384,256]{1,0:T(8,128)(2,1)S(1)} %pad_maximum_fusion), channel_id=1, source_target_pairs={{0,4},{4,8},{8,12},{12,16},{16,20},{20,24},{24,28},{1,5},{5,9},{9,... | collective-permute-start | bytes 589832 | tf_op jit(solution)/shard_map/ppermute | solution.py:15
  68.8 10.7 %collective-permute-start.4 = (bf16[384,256]{1,0:T(8,128)(2,1)S(1)}, bf16[384,256]{1,0:T(8,128)(2,1)S(1)}, u32[]{:S(2)}, u32[]{:S(2)}) collective-permute-start(bf16[384,256]{1,0:T(8,128)(2,1)S(1)} %pad_maximum_fusion), channel_id=1, source_target_pairs={{4,0},{8,4},{12,8},{16,12},{20,16},{24,20},{28,24},{5,1},{9,5},{13... | collective-permute-start | bytes 589832 | tf_op jit(solution)/shard_map/ppermute | solution.py:15
  72.0 8.2 %collective-permute-start.5 = (bf16[384,256]{1,0:T(8,128)(2,1)S(1)}, bf16[384,256]{1,0:T(8,128)(2,1)S(1)}, u32[]{:S(2)}, u32[]{:S(2)}) collective-permute-start(bf16[384,256]{1,0:T(8,128)(2,1)S(1)} %pad_maximum_fusion), channel_id=1, source_target_pairs={{12,0},{16,4},{20,8},{24,12},{28,16},{13,1},{17,5},{21,9},{25,13},... | collective-permute-start | bytes 589832 | tf_op jit(solution)/shard_map/ppermute | solution.py:15
  74.0 12.5 %collective-permute-start.6 = (bf16[384,256]{1,0:T(8,128)(2,1)S(1)}, bf16[384,256]{1,0:T(8,128)(2,1)S(1)}, u32[]{:S(2)}, u32[]{:S(2)}) collective-permute-start(bf16[384,256]{1,0:T(8,128)(2,1)S(1)} %pad_maximum_fusion), channel_id=1, source_target_pairs={{16,0},{20,4},{24,8},{28,12},{17,1},{21,5},{25,9},{29,13},{18,2},{... | collective-permute-start | bytes 589832 | tf_op jit(solution)/shard_map/ppermute | solution.py:15
  76.0 24.1 %collective-permute-start.7 = (bf16[384,256]{1,0:T(8,128)(2,1)S(1)}, bf16[384,256]{1,0:T(8,128)(2,1)S(1)}, u32[]{:S(2)}, u32[]{:S(2)}) collective-permute-start(bf16[384,256]{1,0:T(8,128)(2,1)S(1)} %pad_maximum_fusion), channel_id=1, source_target_pairs={{20,0},{24,4},{28,8},{21,1},{25,5},{29,9},{22,2},{26,6},{30,10},{2... | collective-permute-start | bytes 589832 | tf_op jit(solution)/shard_map/ppermute | solution.py:15
  111.2 1.1 copy-start.2
  112.3 2.3 %copy-start.1 = (f32[384,3456]{1,0:T(8,128)}, f32[384,3456]{1,0:T(8,128)S(1)}, u32[]{:S(2)}) copy-start(f32[384,3456]{1,0:T(8,128)S(1)} %get-tuple-element.12) | copy-start | bytes 15925252
  112.4 2.2 %copy-start.4 = (bf16[256,256]{0,1:T(8,128)(2,1)S(1)}, bf16[256,256]{0,1:T(8,128)(2,1)}, u32[]{:S(2)}) copy-start(bf16[256,256]{0,1:T(8,128)(2,1)} %copy-done.3) | copy-start | bytes 393220
Sparse Core Ops, SparseCore 0:
  9.0 48.1 all-gather.1
  121.9 35.5 reduce-scatter.1
